TPU v7x, 256 devices: a whole 4x4x8 slice. The times are simulated.
256 devices in a mesh: expert: 8 (over y, core), dp: 32 (over x, z).
Axes of the slice: x: 4, y: 4, z: 8, core: 2. Of those that a mesh axis runs over, the one named last changes fastest.
Arguments:
- tokens: bfloat16 [32768, 4096], P(('expert', 'dp')), may hold values from -6 to 6
- gates: float32 [32768, 8], P(('expert', 'dp')), may hold values from 0.05 to 1
- routes: int32 [32768, 8], P(('expert', 'dp')), may hold values from 0 to 127, all different within a row; in each aligned block of 128 rows (0 to 127, 128 to 255, ...) at most 16 rows name the same one
- doc_ids: int32 [32768], P(('expert', 'dp')), may hold values from 0 to 1
- hidden_grad: bfloat16 [128, 4096, 1536], P('expert', 'dp'), may hold values from -6 to 6
- proj_in: bfloat16 [4096, 64], replicated, may hold values from -0.09375 to 0.09375
- proj_out: bfloat16 [128, 1536, 64], P('expert'), may hold values from -0.15625 to 0.15625
- val_features: bfloat16 [128, 128, 4096], P('dp', 'expert'), may hold values from -6 to 6
Outputs:
- scores: float32 [64, 128], P('dp')
Inputs may be any that keep to these rules, and one draw needn't show every extreme that they name: Each row names 8 different experts; among the rows of one device no expert is named by more than 16 routes, and in every draw some expert by exactly 16.
All inputs are finite; a program needn't handle non-finite values.
Results may differ from a plain program's by a relative error of at most 0.0049.
Values may be sent and summed in bfloat16 or wider, within the bound.
A program may use at most 64 MiB of HBM per device.

v0:
```python
import jax
import jax.numpy as jnp
from jax import lax
from jax.sharding import PartitionSpec as P

DOC_GRP = 2


def cut_along(value, dim, devices):
    before, after = (value.shape[:dim], value.shape[dim + 1 :])
    return jnp.moveaxis(value.reshape(*before, devices, -1, *after), dim, 0)


def edges_of(length, count):
    unit = 8 if length >= 8 * count else 1
    return [length // unit * k // count * unit for k in range(1, count)]


def laid_out(parts, dim):
    lengths = list(parts.shape[1:])
    lengths[dim] *= parts.shape[0]
    return jnp.moveaxis(parts, 0, dim).reshape(lengths)


def several_exchanges(value, axis, pieces, split_dim, concat_dim):
    parts = cut_along(value, split_dim, lax.axis_size(axis))
    split_at = max(range(1, max(2, parts.ndim - 1)), key=lambda d: parts.shape[d])
    finished = []
    for slab in jnp.split(parts, edges_of(parts.shape[split_at], pieces), axis=split_at):
        if slab.size:
            finished.append(lax.all_to_all(slab, axis, split_axis=0, concat_axis=0, tiled=True))
    return laid_out(jnp.concatenate(finished, axis=split_at), concat_dim)


def sent_and_summed(value, axis, dim):
    parts = cut_along(value, dim, lax.axis_size(axis))
    arrived = lax.all_to_all(parts, axis, split_axis=0, concat_axis=0, tiled=True)
    return arrived.sum(axis=0)


def sent_to_all(value, axis):
    devices = lax.axis_size(axis)
    return lax.all_to_all(
        jnp.broadcast_to(value[None], (devices, *value.shape)), axis, 0, 0, tiled=True
    )


def taken_together(value, axis):
    everything = sent_to_all(value, axis)
    return jnp.sum(everything, axis=0)


def body(tokens, gates, routes, doc_ids, hidden_grad, proj_in, proj_out, val_features):
    tok_count, top_count = routes.shape
    rank = proj_in.shape[1]
    exp_local = proj_out.shape[0]
    groups = lax.axis_size("expert")
    experts = exp_local * groups
    capacity = hidden_grad.shape[1] // groups
    act = jnp.dot(tokens, proj_in, preferred_element_type=jnp.float32)
    sent = (gates[:, :, None] * act[:, None, :]).astype(jnp.bfloat16).reshape(-1, rank)
    flat_routes = routes.reshape(-1)
    onehot = (flat_routes[:, None] == jnp.arange(experts, dtype=jnp.int32)[None, :]).astype(
        jnp.int32
    )
    prior = jnp.cumsum(onehot, axis=0) - onehot
    slot = jnp.sum(prior * onehot, axis=1)
    index = flat_routes * capacity + slot
    buffer = jnp.zeros((experts * capacity, rank), jnp.bfloat16).at[index].set(sent)
    buffer = buffer.reshape(experts, capacity * rank)
    owners = (
        jnp.full((experts * capacity,), DOC_GRP, jnp.int32)
        .at[index]
        .set(jnp.repeat(doc_ids, top_count))
    )
    owners = owners.reshape(experts, capacity)
    arrived, arrived_docs = (
        lax.all_to_all(buffer, "expert", split_axis=0, concat_axis=1, tiled=True),
        lax.all_to_all(owners, "expert", split_axis=0, concat_axis=1, tiled=True),
    )
    lowered = jnp.einsum(
        "erf,efk->erk", hidden_grad, proj_out, preferred_element_type=jnp.float32
    ).astype(jnp.bfloat16)
    slot_rows = lowered.shape[1]
    arrived = arrived.reshape(exp_local, slot_rows, rank)
    member = (
        arrived_docs[:, :, None] == jnp.arange(DOC_GRP, dtype=jnp.int32)[None, None, :]
    ).astype(jnp.bfloat16)
    spread = (member[:, :, :, None] * arrived[:, :, None, :]).reshape(
        exp_local, slot_rows, DOC_GRP * rank
    )
    features = jnp.einsum("erm,erb->emb", spread, lowered, preferred_element_type=jnp.float32)
    features = features.reshape(exp_local, DOC_GRP, rank * rank).astype(jnp.bfloat16)
    scale = 1.0 / jnp.sqrt(jnp.float32(experts * rank * rank))
    train_share = lax.all_to_all(features, "dp", split_axis=2, concat_axis=1, tiled=True)
    val_share = several_exchanges(val_features, "dp", 2, 2, 0)
    partial_value = jnp.einsum(
        "edk,vek->dv", train_share, val_share, preferred_element_type=jnp.float32
    )
    owned = sent_and_summed(partial_value, "dp", 0)
    summed = taken_together(owned, "expert")
    return summed * scale


def solution(mesh):
    in_specs = (
        P(("expert", "dp"), None),
        P(("expert", "dp"), None),
        P(("expert", "dp"), None),
        P(("expert", "dp")),
        P("expert", "dp", None),
        P(),
        P("expert", None, None),
        P("dp", "expert", None),
    )
    out_specs = P("dp", None)
    return jax.shard_map(body, mesh=mesh, in_specs=in_specs, out_specs=out_specs, check_vma=False)
```

profile of v0, /device:TPU:1, one launch (start us, length us, event | category | flops | bytes accessed | tf_op | source)
XLA Modules:
  0.0 138.3 jit_solution(3329710281538476307)
XLA Ops:
  5.3 1.4 %fusion.1 = s32[1024]{0:T(1024)S(1)} fusion(s32[128,8,128]{0,2,1:T(8,128)} %copy.120, s32[1024]{0:T(1024)S(1)} %eq.44), kind=kLoop, calls=%fused_computation.9 | loop fusion | flops 654336 | bytes 532480 | tf_op jit(solution)/shard_map/reduce_sum | solution.py:67
  6.8 4.3 %scatter_custom_fusion = s32[2048]{0:T(1024)S(1)} fusion(s32[1024]{0:T(1024)S(1)} %bitcast.60, s32[1024]{0:T(1024)S(1)} %reshape.96, s32[]{:T(128)} %constant.7.clone.1), kind=kCustom, calls=%fused_computation.27 | custom fusion | bytes 8196 | tf_op jit(solution)/shard_map/scatter | solution.py:74
  11.9 6.4 %all-to-all-start = ((s32[8,1,256]{2,1,0:T(1,128)}), s32[8,1,256]{2,1,0:T(1,128)S(1)}, u32[]{:S(2)}, u32[]{:S(2)}) async-start(s32[8,1,256]{2,1,0:T(1,128)} %reshape.114), calls=%async_computation | async-start | bytes 16384 | tf_op jit(solution)/shard_map/all_to_all | solution.py:79
  19.4 1.8 %fusion.15 = f32[128,64]{1,0:T(8,128)S(1)} fusion(bf16[128,4096]{1,0:T(8,128)(2,1)} %param.8, bf16[4096,64]{0,1:T(8,128)(2,1)} %param.13), kind=kOutput, calls=%fused_computation.32 | convolution fusion | flops 67108864 | bytes 1605632 | tf_op jit(solution)/shard_map/dot_general | solution.py:60
  22.2 4.5 %scatter_custom_fusion.1 = bf16[2048,64]{1,0:T(8,128)(2,1)} fusion(s32[1024]{0:T(1024)S(1)} %bitcast.61, f32[128,64]{1,0:T(8,128)S(1)} %fusion.15, f32[1024]{0:T(1024)S(1)} %mul.67, bf16[]{:T(256)} %constant.5.clone.1), kind=kCustom, calls=%fused_computation.16 | custom fusion | flops 131072 | bytes 331778 | tf_op jit(solution)/shard_map/scatter | solution.py:69
  26.7 2.2 %all_to_all.52 = bf16[8,16,1024]{2,1,0:T(8,128)(2,1)} reshape(bf16[2048,64]{1,0:T(8,128)(2,1)} %scatter_custom_fusion.1) | data formatting | bytes 524288 | tf_op jit(solution)/shard_map/all_to_all | solution.py:78
  28.9 4.8 %all-to-all-start.1 = ((bf16[8,16,1024]{2,1,0:T(8,128)(2,1)}), bf16[8,16,1024]{2,1,0:T(8,128)(2,1)S(1)}, u32[]{:S(2)}, u32[]{:S(2)}) async-start(bf16[8,16,1024]{2,1,0:T(8,128)(2,1)} %all_to_all.52), calls=%async_computation.1 | async-start | bytes 524288 | tf_op jit(solution)/shard_map/all_to_all | solution.py:78
  33.7 1.8 %fusion.14 = (bf16[32,4,8,128]{3,0,2,1:T(8,128)(2,1)S(1)}, bf16[32,4,8,128]{3,0,2,1:T(8,128)(2,1)}) fusion(bf16[32,4,16,128]{3,0,2,1:T(8,128)(2,1)} %bitcast_bitcast_fusion), kind=kLoop, calls=%fused_computation.31 | loop fusion | bytes 1048576 | tf_op jit(solution)/shard_map/split | solution.py:29
  36.4 3.8 %all-to-all-done.1 = bf16[8,16,1024]{2,1,0:T(8,128)(2,1)S(1)} async-done(((bf16[8,16,1024]{2,1,0:T(8,128)(2,1)}), bf16[8,16,1024]{2,1,0:T(8,128)(2,1)S(1)}, u32[]{:S(2)}, u32[]{:S(2)}) %all-to-all-start.1) | async-done | bytes 262176 | tf_op jit(solution)/shard_map/all_to_all | solution.py:78
  40.2 10.7 %all-to-all-start.3 = ((bf16[32,4,8,128]{3,1,2,0:T(4,128)(2,1)}), bf16[32,4,8,128]{3,1,2,0:T(4,128)(2,1)}, u32[]{:S(2)}, u32[]{:S(2)}) async-start(bf16[32,4,8,128]{3,1,2,0:T(4,128)(2,1)} %copy.131), calls=%async_computation.3 | async-start | bytes 524288 | tf_op jit(solution)/shard_map/all_to_all | solution.py:31
  50.9 1.9 %copy.132 = bf16[32,4,8,128]{3,1,2,0:T(4,128)(2,1)} copy(bf16[32,4,8,128]{3,0,2,1:T(8,128)(2,1)} %get-tuple-element.6) | data formatting | bytes 524288 | tf_op jit(solution)/shard_map/split | solution.py:29
  58.5 2.1 %all-to-all-done.3 = bf16[32,4,8,128]{3,1,2,0:T(4,128)(2,1)} async-done(((bf16[32,4,8,128]{3,1,2,0:T(4,128)(2,1)}), bf16[32,4,8,128]{3,1,2,0:T(4,128)(2,1)}, u32[]{:S(2)}, u32[]{:S(2)}) %all-to-all-start.3) | async-done | bytes 262176 | tf_op jit(solution)/shard_map/all_to_all | solution.py:31
  60.6 7.4 %all-to-all-start.4 = ((bf16[32,4,8,128]{3,1,2,0:T(4,128)(2,1)}), bf16[32,4,8,128]{3,1,2,0:T(4,128)(2,1)}, u32[]{:S(2)}, u32[]{:S(2)}) async-start(bf16[32,4,8,128]{3,1,2,0:T(4,128)(2,1)} %copy.132), calls=%async_computation.4 | async-start | bytes 524288 | tf_op jit(solution)/shard_map/all_to_all | solution.py:31
  68.0 5.5 %convolution_convert_fusion = bf16[16,128,64]{1,2,0:T(8,128)(2,1)S(1)} fusion(bf16[16,128,128]{1,2,0:T(8,128)(2,1)} %bitcast.53, bf16[16,128,1536]{2,1,0:T(8,128)(2,1)} %param.12, bf16[16,1536,64]{1,2,0:T(8,128)(2,1)S(1)} %copy-done), kind=kOutput, calls=%fused_computation.2 | convolution fusion | flops 436469760 | bytes 10223616 | tf_op jit(solution)/shard_map/erm,erb->emb/dot_general | solution.py:92
  74.5 1.4 %convert_element_type.33 = bf16[16,2,4096]{2,1,0:T(2,128)(2,1)S(1)} reshape(bf16[16,128,64]{2,1,0:T(8,128)(2,1)} %copy.127) | data formatting | bytes 524288 | tf_op jit(solution)/shard_map/convert_element_type | solution.py:93
  76.0 3.8 %copy.128 = bf16[16,2,4096]{0,1,2:T(2,128)(2,1)} copy(bf16[16,2,4096]{2,1,0:T(2,128)(2,1)S(1)} %convert_element_type.33) | data formatting | bytes 524288 | tf_op jit(solution)/shard_map/convert_element_type | solution.py:93
  79.8 7.3 %reshape.116 = bf16[32,2,2048]{2,1,0:T(2,128)(2,1)} reshape(bf16[4096,2,16]{2,1,0:T(2,128)(2,1)} %bitcast.51) | data formatting | bytes 524288
  87.1 9.0 %all-to-all-start.2 = ((bf16[32,2,2048]{2,1,0:T(2,128)(2,1)}), bf16[32,2,2048]{2,1,0:T(2,128)(2,1)S(1)}, u32[]{:S(2)}, u32[]{:S(2)}) async-start(bf16[32,2,2048]{2,1,0:T(2,128)(2,1)} %reshape.116), calls=%async_computation.2 | async-start | bytes 524288 | tf_op jit(solution)/shard_map/all_to_all | solution.py:95
  96.1 1.4 pad_maximum_fusion
  98.5 7.2 %all-to-all-done.2 = bf16[32,2,2048]{2,1,0:T(2,128)(2,1)S(1)} async-done(((bf16[32,2,2048]{2,1,0:T(2,128)(2,1)}), bf16[32,2,2048]{2,1,0:T(2,128)(2,1)S(1)}, u32[]{:S(2)}, u32[]{:S(2)}) %all-to-all-start.2) | async-done | bytes 262176 | tf_op jit(solution)/shard_map/all_to_all | solution.py:95
  105.8 2.4 %reshape.117 = bf16[4096,2,16]{2,1,0:T(2,128)(2,1)} reshape(bf16[32,2,2048]{2,1,0:T(2,128)(2,1)S(1)} %all-to-all-done.2) | data formatting | bytes 524288
  108.2 3.2 %copy.142 = bf16[16,2,32,128]{3,2,0,1:T(8,128)(2,1)S(1)} copy(bf16[16,2,32,128]{0,1,3,2:T(2,128)(2,1)} %bitcast.52) | data formatting | bytes 524288 | tf_op jit(solution)/shard_map/edk,vek->dv/dot_general | solution.py:97
  112.8 13.2 %all_to_all.70 = f32[32,2,128]{2,1,0:T(2,128)S(1)} all-to-all(f32[32,2,128]{2,1,0:T(2,128)S(1)} %copy.135), channel_id=1, replica_groups=mesh['expert'=8,'dp'=32] {'dp'}, dimensions={0} | all-to-all | bytes 65536 | tf_op jit(solution)/shard_map/all_to_all | solution.py:37
  126.1 11.7 %all_to_all.71 = f32[8,2,128]{2,1,0:T(2,128)S(1)} all-to-all(f32[8,2,128]{2,1,0:T(2,128)S(1)} %broadcast_in_dim.11), channel_id=1, replica_groups=mesh['expert'=8,'dp'=32] {'expert'}, dimensions={0} | all-to-all | bytes 16384 | tf_op jit(solution)/shard_map/all_to_all | solution.py:43
  (53 shorter events, 18.9 us)
Async XLA Ops:
  0.0 68.0 %copy-start = (bf16[16,1536,64]{1,2,0:T(8,128)(2,1)S(1)}, bf16[16,1536,64]{1,2,0:T(8,128)(2,1)}, u32[]{:S(2)}) copy-start(bf16[16,1536,64]{1,2,0:T(8,128)(2,1)} %param.14) | copy-start | bytes 9437188
  0.0 5.1 %copy-start.4 = (s32[128]{0:T(128)S(1)}, s32[128]{0:T(128)}, u32[]{:S(2)}) copy-start(s32[128]{0:T(128)} %param.11) | copy-start | bytes 1540
  2.1 0.8 copy-start.1
  4.0 18.0 %copy-start.3 = (f32[128,8]{0,1:T(8,128)S(1)}, f32[128,8]{0,1:T(8,128)}, u32[]{:S(2)}) copy-start(f32[128,8]{0,1:T(8,128)} %param.9) | copy-start | bytes 12292
  11.9 17.0 %all-to-all-start = ((s32[8,1,256]{2,1,0:T(1,128)}), s32[8,1,256]{2,1,0:T(1,128)S(1)}, u32[]{:S(2)}, u32[]{:S(2)}) async-start(s32[8,1,256]{2,1,0:T(1,128)} %reshape.114), calls=%async_computation | async-start | bytes 16384 | tf_op jit(solution)/shard_map/all_to_all | solution.py:79
  28.9 11.3 %all-to-all-start.1 = ((bf16[8,16,1024]{2,1,0:T(8,128)(2,1)}), bf16[8,16,1024]{2,1,0:T(8,128)(2,1)S(1)}, u32[]{:S(2)}, u32[]{:S(2)}) async-start(bf16[8,16,1024]{2,1,0:T(8,128)(2,1)} %all_to_all.52), calls=%async_computation.1 | async-start | bytes 524288 | tf_op jit(solution)/shard_map/all_to_all | solution.py:78
  40.2 14.0 %copy-start.2 = (bf16[8,16,1024]{2,1,0:T(8,128)(2,1)}, bf16[8,16,1024]{2,1,0:T(8,128)(2,1)S(1)}, u32[]{:S(2)}) copy-start(bf16[8,16,1024]{2,1,0:T(8,128)(2,1)S(1)} %all-to-all-done.1) | copy-start | bytes 786436
  40.2 20.3 %all-to-all-start.3 = ((bf16[32,4,8,128]{3,1,2,0:T(4,128)(2,1)}), bf16[32,4,8,128]{3,1,2,0:T(4,128)(2,1)}, u32[]{:S(2)}, u32[]{:S(2)}) async-start(bf16[32,4,8,128]{3,1,2,0:T(4,128)(2,1)} %copy.131), calls=%async_computation.3 | async-start | bytes 524288 | tf_op jit(solution)/shard_map/all_to_all | solution.py:31
  60.6 26.6 %all-to-all-start.4 = ((bf16[32,4,8,128]{3,1,2,0:T(4,128)(2,1)}), bf16[32,4,8,128]{3,1,2,0:T(4,128)(2,1)}, u32[]{:S(2)}, u32[]{:S(2)}) async-start(bf16[32,4,8,128]{3,1,2,0:T(4,128)(2,1)} %copy.132), calls=%async_computation.4 | async-start | bytes 524288 | tf_op jit(solution)/shard_map/all_to_all | solution.py:31
  87.1 18.6 %all-to-all-start.2 = ((bf16[32,2,2048]{2,1,0:T(2,128)(2,1)}), bf16[32,2,2048]{2,1,0:T(2,128)(2,1)S(1)}, u32[]{:S(2)}, u32[]{:S(2)}) async-start(bf16[32,2,2048]{2,1,0:T(2,128)(2,1)} %reshape.116), calls=%async_computation.2 | async-start | bytes 524288 | tf_op jit(solution)/shard_map/all_to_all | solution.py:95
where the time goes:
time: 139 us; the launch traced here: 138 us
  local copies, waits for them, and re-layouts  41.7 us (30%)
  starting transfers between devices  38.3 us (28%)
  blocking collectives  24.9 us (18%)
  waiting for transfers between devices  13.1 us (9%)
  other arithmetic  11.4 us (8%)
  matrix products  8.65 us (6%)
    all_to_all x2, starting transfers between devices, several_exchanges(): lax.all_to_all(slab, axis, split_axis=0, concat_axis=0, tiled=True)  18.1 us
    unnamed x17, local copies, waits for them, and re-layouts  13.5 us
    all_to_all x1, blocking collectives, sent_and_summed(): lax.all_to_all(parts, axis, split_axis=0, concat_axis=0, tiled=True)  13.2 us
    all_to_all x1, blocking collectives, sent_to_all(): lax.all_to_all(jnp.broadcast_to(value[None], (devices, *value.shape)), ax...  11.7 us
    all_to_all x1, starting transfers between devices, body(): lax.all_to_all(features, 'dp', split_axis=2, concat_axis=1, tiled=True)  8.98 us
    all_to_all x1, waiting for transfers between devices, body(): lax.all_to_all(features, 'dp', split_axis=2, concat_axis=1, tiled=True)  7.22 us
    all_to_all x1, starting transfers between devices, body(): lax.all_to_all(owners, 'expert', split_axis=0, concat_axis=1, tiled=True)  6.43 us
    convert_element_type x3, local copies, waits for them, and re-layouts, body(): features.reshape(exp_local, DOC_GRP, rank * rank).astype(jnp.bfloat16)  6.26 us
  transfers between devices with their start and end apart: 5, of which 3 were waited for; matrix products, arithmetic and copies ran while one was open for 29% of the time, Pallas kernels for 0%

commit v1 on v0

v1 whole, which is shorter than its diff:
```python
import functools

import jax
import jax.numpy as jnp
from jax import lax
from jax.experimental import pallas as pl
from jax.experimental.pallas import tpu as pltpu
from jax.sharding import PartitionSpec as P

MESH = pl.DeviceIdType.MESH
BF = jnp.bfloat16
F32 = jnp.float32
NT = (((1,), (1,)), ((), ()))


def iota(shape, dim):
    return lax.broadcasted_iota(jnp.int32, shape, dim)


def dot(a, b):
    return jnp.dot(a, b, preferred_element_type=F32)


def dot_nt(a, b):
    return lax.dot_general(a, b, NT, preferred_element_type=F32)


def whole(ref, sem):
    pltpu.make_async_copy(ref, ref, sem).wait()


def kernel(
    n_dp, n_ex,
    tok_hbm, gate_hbm, route_hbm, doc_hbm, grad_hbm, pin_hbm, pout_hbm, val_hbm,
    out_ref,
    tok, gate, route, doc, grad, pin, pout,
    slots, gated, ysend, yrecv, diag, feats, raw, vals, train, part, owned, total, mine,
    in_sem, pair_sem, val_s, val_r, act_s, act_r, train_s, train_r, part_s, part_r, own_s, own_r,
):
    me = lax.axis_index("dp")
    ex = lax.axis_index("expert")

    def dp_at(k):
        return lax.rem(me + k, n_dp)

    def ex_at(k):
        return lax.rem(ex + k, n_ex)

    loads = [
        pltpu.make_async_copy(src, dst, in_sem.at[n])
        for n, (src, dst) in enumerate(
            [(route_hbm, route), (gate_hbm, gate), (doc_hbm, doc), (pin_hbm, pin), (tok_hbm, tok)]
        )
    ]
    for load in loads:
        load.start()

    def pair_loads(c):
        rows, cols = pl.ds(pl.multiple_of(c * 256, 256), 256), pl.ds(pl.multiple_of(c * 128, 128), 128)
        return (
            pltpu.make_async_copy(grad_hbm.at[rows], grad.at[rows], pair_sem.at[0, c]),
            pltpu.make_async_copy(pout_hbm.at[cols], pout.at[cols], pair_sem.at[1, c]),
        )

    barrier = pltpu.get_barrier_semaphore()

    @pl.loop(1, n_dp)
    def _(k):
        pl.semaphore_signal(barrier, inc=1, device_id=(ex, dp_at(k)), device_id_type=MESH)

    @pl.loop(1, n_ex)
    def _(k):
        pl.semaphore_signal(barrier, inc=1, device_id=(ex_at(k), me), device_id_type=MESH)

    @pl.loop(0, 8)
    def _(c):
        for load in pair_loads(c):
            load.start()

    for load in loads[:3]:
        load.wait()
    experts = iota((128, 128), 0)
    named = jnp.zeros((128, 128), F32)
    weight = jnp.zeros((128, 128), F32)
    for k in range(8):
        hit = route[k : k + 1, :] == experts
        named = jnp.where(hit, 1.0, named)
        weight = jnp.where(hit, gate[k : k + 1, :], weight)
    earlier = (iota((128, 128), 0) < iota((128, 128), 1)).astype(BF)
    slots[...] = jnp.where(named > 0.0, dot(named.astype(BF), earlier), -1.0)
    gated[...] = weight

    @pl.loop(0, 16)
    def _(r):
        diag[:, pl.ds(pl.multiple_of(r * 64, 64), 64), :] = jnp.zeros((2, 64, 512), BF)

    for load in loads[3:]:
        load.wait()
    act = dot_nt(pin[...], tok[...])
    act_hi = act.astype(BF)
    act_lo = (act - act_hi.astype(F32)).astype(BF)
    row, col = iota((128, 64), 0), iota((128, 64), 1)
    spread = (col == 2 * ((row % 64) // 2) + row // 64).astype(BF)
    member = iota((128, 128), 0) % 2 == doc[...]
    x_hi = jnp.where(member, dot(spread, act_hi), 0.0).astype(BF)
    x_lo = jnp.where(member, dot(spread, act_lo), 0.0).astype(BF)

    place = iota((16, 128), 0).astype(F32)

    @pl.loop(0, n_ex)
    def _(g):
        blocks = []
        for e in range(16):
            at = pl.ds(g * 16 + e, 1)
            blocks.append(jnp.where(slots[at, :] == place, gated[at, :], 0.0))
        pick = jnp.concatenate(blocks, axis=0)
        pick_hi = pick.astype(BF)
        pick_lo = (pick - pick_hi.astype(F32)).astype(BF)
        y = dot_nt(x_hi, pick_hi) + dot_nt(x_lo, pick_hi) + dot_nt(x_hi, pick_lo)
        y = y.astype(BF)
        ysend[g, 0] = y[:, :128]
        ysend[g, 1] = y[:, 128:]

    pl.semaphore_wait(barrier, n_dp - 1 + n_ex - 1)

    def act_dst():
        return yrecv.at[:, :, pl.ds(pl.multiple_of(ex * 128, 128), 128)]

    @pl.loop(1, n_ex)
    def _(k):
        to = ex_at(k)
        pltpu.make_async_remote_copy(
            ysend.at[to], act_dst(), act_s, act_r, device_id=(to, me), device_id_type=MESH
        ).start()

    pltpu.make_async_copy(ysend.at[ex], act_dst(), act_r).start()

    def val_src(to):
        return val_hbm.at[:, :, pl.ds(pl.multiple_of(to * 128, 128), 128)]

    def val_dst():
        return raw.at[pl.ds(me * 4, 4)]

    @pl.loop(1, n_dp)
    def _(k):
        to = dp_at(k)
        pltpu.make_async_remote_copy(
            val_src(to), val_dst(), val_s, val_r, device_id=(ex, to), device_id_type=MESH
        ).start()

    pltpu.make_async_copy(val_src(me), val_dst(), val_r).start()

    own_half = (iota((256, 128), 0) // 128) == (iota((256, 128), 1) // 64)

    @pl.loop(0, 8)
    def _(c):
        for load in pair_loads(c):
            load.wait()
        both = dot_nt(
            grad[pl.ds(pl.multiple_of(c * 256, 256), 256), :],
            pout[pl.ds(pl.multiple_of(c * 128, 128), 128), :],
        )
        both = jnp.where(own_half, both, 0.0).astype(BF)
        half, inner = c // 4, lax.rem(c, 4)
        cols = pl.ds(pl.multiple_of(inner * 128, 128), 128)
        for i in range(8):
            for e in range(2):
                rows = pl.ds(pl.multiple_of(i * 128 + inner * 32 + e * 16, 16), 16)
                diag[half, rows, cols] = both[e * 128 + i * 16 : e * 128 + i * 16 + 16, :]

    whole(yrecv, act_r)
    low = iota((64, 128), 1) < 64

    @pl.loop(0, 4)
    def _(q):
        half, inner = q // 2, lax.rem(q, 2)
        cols = pl.ds(pl.multiple_of(inner * 256, 256), 256)
        f = dot(yrecv[half], diag[half, :, cols])
        for h in range(2):
            even, odd = f[:64, h * 128 : h * 128 + 128], f[64:, h * 128 : h * 128 + 128]
            feats[4 * q + 2 * h] = jnp.where(low, even, pltpu.roll(odd, 64, 1)).astype(BF)
            feats[4 * q + 2 * h + 1] = jnp.where(low, pltpu.roll(even, 64, 1), odd).astype(BF)

    def pair(ref, at):
        return ref.at[:, pl.ds(at * 2, 2), :]

    @pl.loop(1, n_dp)
    def _(k):
        to = dp_at(k)
        pltpu.make_async_remote_copy(
            pair(feats, to), pair(train, me), train_s, train_r, device_id=(ex, to), device_id_type=MESH
        ).start()

    pltpu.make_async_copy(pair(feats, me), pair(train, me), train_r).start()

    row, col = iota((256, 256), 0), iota((256, 256), 1)
    swap = ((row // 16 == col % 16) & (row % 16 == col // 16)).astype(BF)
    whole(raw, val_r)

    @pl.loop(0, 8)
    def _(b):
        at = pl.ds(pl.multiple_of(b * 16, 16), 16)
        turned = dot(swap, raw[at].reshape(256, 128)).astype(BF)
        for e in range(16):
            vals[e, at, :] = turned[e * 16 : e * 16 + 16, :]

    whole(train, train_r)
    score = jnp.zeros((64, 128), F32)
    for e in range(16):
        score += dot_nt(train[e], vals[e])
    part[...] = score

    def two(ref, at):
        return ref.at[pl.ds(at * 2, 2), :]

    @pl.loop(1, n_dp)
    def _(k):
        to = dp_at(k)
        pltpu.make_async_remote_copy(
            two(part, to), two(owned, me), part_s, part_r, device_id=(ex, to), device_id_type=MESH
        ).start()

    pltpu.make_async_copy(two(part, me), two(owned, me), part_r).start()
    whole(owned, part_r)

    def folded(value):
        value = value + pltpu.roll(value, 4, 0)
        return value + pltpu.roll(value, 2, 0)

    rows = owned[0:8, :]
    for n in range(1, 8):
        rows += owned[8 * n : 8 * n + 8, :]
    mine[...] = folded(rows)

    @pl.loop(1, n_ex)
    def _(k):
        pltpu.make_async_remote_copy(
            mine.at[0:2, :], two(total, ex), own_s, own_r, device_id=(ex_at(k), me), device_id_type=MESH
        ).start()

    pltpu.make_async_copy(mine.at[0:2, :], two(total, ex), own_r).start()
    whole(total, own_r)
    out_ref[...] = folded(total[0:8, :] + total[8:16, :])[0:2, :]

    whole(yrecv.at[:, :, 0:896], act_s)
    whole(raw.at[0:124], val_s)
    whole(train.at[:, 0:62, :], train_s)
    whole(owned.at[0:62, :], part_s)
    whole(total.at[0:14, :], own_s)


def body(tokens, gates, routes, doc_ids, hidden_grad, proj_in, proj_out, val_features):
    n_dp, n_ex = lax.axis_size("dp"), lax.axis_size("expert")
    entries = proj_out.shape[0] * n_ex * proj_in.shape[1] ** 2
    dma = pltpu.SemaphoreType.DMA
    summed = pl.pallas_call(
        functools.partial(kernel, n_dp, n_ex),
        out_shape=jax.ShapeDtypeStruct((2, 128), F32),
        in_specs=[pl.BlockSpec(memory_space=pltpu.HBM)] * 8,
        out_specs=pl.BlockSpec(memory_space=pltpu.VMEM),
        scratch_shapes=[
            pltpu.VMEM((128, 4096), BF),
            pltpu.VMEM((8, 128), F32),
            pltpu.VMEM((8, 128), jnp.int32),
            pltpu.VMEM((1, 128), jnp.int32),
            pltpu.VMEM((2048, 1536), BF),
            pltpu.VMEM((64, 4096), BF),
            pltpu.VMEM((1024, 1536), BF),
            pltpu.VMEM((128, 128), F32),
            pltpu.VMEM((128, 128), F32),
            pltpu.VMEM((8, 2, 128, 128), BF),
            pltpu.VMEM((2, 128, 1024), BF),
            pltpu.VMEM((2, 1024, 512), BF),
            pltpu.VMEM((16, 64, 128), BF),
            pltpu.VMEM((128, 16, 128), BF),
            pltpu.VMEM((16, 128, 128), BF),
            pltpu.VMEM((16, 64, 128), BF),
            pltpu.VMEM((64, 128), F32),
            pltpu.VMEM((64, 128), F32),
            pltpu.VMEM((16, 128), F32),
            pltpu.VMEM((8, 128), F32),
            dma((5,)),
            dma((2, 8)),
        ]
        + [dma] * 10,
        compiler_params=pltpu.CompilerParams(
            collective_id=0, has_side_effects=True, vmem_limit_bytes=48 << 20
        ),
    )(
        tokens,
        gates.T,
        routes.T,
        doc_ids.reshape(1, -1),
        hidden_grad.reshape(-1, hidden_grad.shape[2]),
        proj_in.T,
        jnp.swapaxes(proj_out, 1, 2).reshape(-1, proj_out.shape[1]),
        val_features,
    )
    return summed * (1.0 / jnp.sqrt(F32(entries)))


def solution(mesh):
    in_specs = (
        P(("expert", "dp"), None),
        P(("expert", "dp"), None),
        P(("expert", "dp"), None),
        P(("expert", "dp")),
        P("expert", "dp", None),
        P(),
        P("expert", None, None),
        P("dp", "expert", None),
    )
    return jax.shard_map(body, mesh=mesh, in_specs=in_specs, out_specs=P("dp", None), check_vma=False)
```

time: 139 us -> 50.7 us (0.36)
  Pallas kernels: 0 us -> 42.6 us
  starting transfers between devices: 38.3 us -> 0 us
  local copies, waits for them, and re-layouts: 41.7 us -> 7.22 us
  blocking collectives: 24.9 us -> 0 us
  waiting for transfers between devices: 13.1 us -> 0 us
  other arithmetic: 11.4 us -> 0.56 us
  matrix products: 8.65 us -> 0 us
    pallas_call x0 -> x1, Pallas kernels: none -> 42.6 us  [body(): pl.pallas_call(functools.partial(kernel, n_dp, n_ex), out_shape=jax.Shape...]
    all_to_all x5 -> x0, starting transfers between devices: 38.3 us -> none  [the longest x2 18.1 us: several_exchanges(): lax.all_to_all(slab, axis, split_axis=0, concat_axis=0, tiled=True)]
    all_to_all x2 -> x0, blocking collectives: 24.9 us -> none  [the longest x1 13.2 us: sent_and_summed(): lax.all_to_all(parts, axis, split_axis=0, concat_axis=0, tiled=True)]
    all_to_all x5 -> x0, waiting for transfers between devices: 13.1 us -> none  [the longest x1 7.22 us: body(): lax.all_to_all(features, 'dp', split_axis=2, concat_axis=1, tiled=True)]
    dot_general x3 -> x0, matrix products: 8.65 us -> none  [the longest x1 5.53 us: body(): jnp.einsum('erm,erb->emb', spread, lowered, preferred_element_type=jnp.fl...]
    unnamed x17 -> x14, local copies, waits for them, and re-layouts: 13.5 us -> 7.22 us
    convert_element_type x3 -> x0, local copies, waits for them, and re-layouts: 6.26 us -> none  [body(): features.reshape(exp_local, DOC_GRP, rank * rank).astype(jnp.bfloat16)]
    split x3 -> x0, local copies, waits for them, and re-layouts: 4.54 us -> none  [several_exchanges(): jnp.split(parts, edges_of(parts.shape[split_at], pieces), axis=split_at)]
  transfers between devices with their start and end apart: 5 -> 0, of which waited for: 3 -> 0; matrix products, arithmetic and copies ran while one was open for 29% -> 0% of each run, Pallas kernels for 0% -> 0%
where the time goes in v1:
time: 50.7 us; the launch traced here: 50.4 us
  Pallas kernels  42.6 us (84%)
  local copies, waits for them, and re-layouts  7.22 us (14%)
  other arithmetic  0.56 us (1%)
    pallas_call x1, Pallas kernels, body(): pl.pallas_call(functools.partial(kernel, n_dp, n_ex), out_shape=jax.Shape...  42.6 us
    unnamed x14, local copies, waits for them, and re-layouts  7.22 us

profile of v1, /device:TPU:1, one launch (start us, length us, event | category | flops | bytes accessed | tf_op | source)
XLA Modules:
  0.0 50.4 jit_solution(5444138387821749751)
XLA Ops:
  0.0 0.0 copy-start
  0.0 1.9 %copy-done = bf16[16,1536,64]{1,2,0:T(8,128)(2,1)S(1)} copy-done((bf16[16,1536,64]{1,2,0:T(8,128)(2,1)S(1)}, bf16[16,1536,64]{1,2,0:T(8,128)(2,1)}, u32[]{:S(2)}) %copy-start) | copy-done | bytes 3145752
  1.9 0.0 copy-start.1
  1.9 1.2 %copy-done.1 = bf16[128,4096]{1,0:T(8,128)(2,1)S(1)} copy-done((bf16[128,4096]{1,0:T(8,128)(2,1)S(1)}, bf16[128,4096]{1,0:T(8,128)(2,1)}, u32[]{:S(2)}) %copy-start.1) | copy-done | bytes 1048600
  3.1 0.0 copy-start.2
  3.1 1.0 %copy-done.2 = bf16[4096,64]{0,1:T(8,128)(2,1)S(1)} copy-done((bf16[4096,64]{0,1:T(8,128)(2,1)S(1)}, bf16[4096,64]{0,1:T(8,128)(2,1)}, u32[]{:S(2)}) %copy-start.2) | copy-done | bytes 524312
  4.2 0.0 copy-start.3
  4.2 1.0 %copy-done.3 = bf16[4,16,4096]{2,1,0:T(8,128)(2,1)S(1)} copy-done((bf16[4,16,4096]{2,1,0:T(8,128)(2,1)S(1)}, bf16[4,16,4096]{2,1,0:T(8,128)(2,1)}, u32[]{:S(2)}) %copy-start.3) | copy-done | bytes 524312
  5.2 0.0 copy-start.4
  5.2 0.7 %copy-done.4 = f32[128,8]{0,1:T(8,128)S(1)} copy-done((f32[128,8]{0,1:T(8,128)S(1)}, f32[128,8]{0,1:T(8,128)}, u32[]{:S(2)}) %copy-start.4) | copy-done | bytes 4120
  5.9 0.0 copy-start.5
  5.9 0.7 %copy-done.5 = s32[128,8]{0,1:T(8,128)S(1)} copy-done((s32[128,8]{0,1:T(8,128)S(1)}, s32[128,8]{0,1:T(8,128)}, u32[]{:S(2)}) %copy-start.5) | copy-done | bytes 4120
  6.6 0.0 copy-start.6
  6.6 0.7 %copy-done.6 = s32[128]{0:T(128)S(1)} copy-done((s32[128]{0:T(128)S(1)}, s32[128]{0:T(128)}, u32[]{:S(2)}) %copy-start.6) | copy-done | bytes 536
  7.2 42.6 %shard_map.82 = f32[2,128]{1,0:T(2,128)S(1)} custom-call(bf16[128,4096]{1,0:T(8,128)(2,1)S(1)} %copy-done.1, f32[8,128]{1,0:T(8,128)S(1)} %bitcast.10, s32[8,128]{1,0:T(8,128)S(1)} %bitcast.11, s32[1,128]{1,0:T(1,128)S(1)} %bitcast.12, bf16[2048,1536]{1,0:T(8,128)(2,1)} %bitcast.13, bf16[64,4096]{1,0:T(8,128)(2,1)S(1)} %bitcast.9, ...), custom_call_target="tpu_custom_call" | custom-call | tf_op jit(solution)/shard_map/pallas_call | solution.py:256
  49.8 0.6 %broadcast_multiply_fusion = f32[2,128]{1,0:T(2,128)} fusion(f32[2,128]{1,0:T(2,128)S(1)} %shard_map.82), kind=kLoop, calls=%fused_computation | loop fusion | flops 256 | bytes 2048 | tf_op jit(solution)/shard_map/mul | solution.py:299
Async XLA Ops:
  0.0 1.9 %copy-start = (bf16[16,1536,64]{1,2,0:T(8,128)(2,1)S(1)}, bf16[16,1536,64]{1,2,0:T(8,128)(2,1)}, u32[]{:S(2)}) copy-start(bf16[16,1536,64]{1,2,0:T(8,128)(2,1)} %param.14) | copy-start | bytes 9437188
  1.9 1.2 %copy-start.1 = (bf16[128,4096]{1,0:T(8,128)(2,1)S(1)}, bf16[128,4096]{1,0:T(8,128)(2,1)}, u32[]{:S(2)}) copy-start(bf16[128,4096]{1,0:T(8,128)(2,1)} %tok_hbm.1) | copy-start | bytes 3145732
  3.1 1.0 %copy-start.2 = (bf16[4096,64]{0,1:T(8,128)(2,1)S(1)}, bf16[4096,64]{0,1:T(8,128)(2,1)}, u32[]{:S(2)}) copy-start(bf16[4096,64]{0,1:T(8,128)(2,1)} %param.13) | copy-start | bytes 1572868
  4.2 1.0 %copy-start.3 = (bf16[4,16,4096]{2,1,0:T(8,128)(2,1)S(1)}, bf16[4,16,4096]{2,1,0:T(8,128)(2,1)}, u32[]{:S(2)}) copy-start(bf16[4,16,4096]{2,1,0:T(8,128)(2,1)} %val_hbm.1) | copy-start | bytes 1572868
  5.2 0.7 %copy-start.4 = (f32[128,8]{0,1:T(8,128)S(1)}, f32[128,8]{0,1:T(8,128)}, u32[]{:S(2)}) copy-start(f32[128,8]{0,1:T(8,128)} %param.9) | copy-start | bytes 12292
  5.9 0.7 %copy-start.5 = (s32[128,8]{0,1:T(8,128)S(1)}, s32[128,8]{0,1:T(8,128)}, u32[]{:S(2)}) copy-start(s32[128,8]{0,1:T(8,128)} %param.10) | copy-start | bytes 12292
  6.6 0.7 %copy-start.6 = (s32[128]{0:T(128)S(1)}, s32[128]{0:T(128)}, u32[]{:S(2)}) copy-start(s32[128]{0:T(128)} %param.11) | copy-start | bytes 1540

commit v2 on v1

--- a/solution.py
+++ b/solution.py
@@ -11,6 +11,7 @@
 BF = jnp.bfloat16
 F32 = jnp.float32
 NT = (((1,), (1,)), ((), ()))
+RING_Z = 8
 
 
 def iota(shape, dim):
@@ -40,11 +41,27 @@
     me = lax.axis_index("dp")
     ex = lax.axis_index("expert")
 
+    def outward(k, n):
+        return n // 2 + jnp.where(lax.rem(k, 2) == 0, k // 2, -((k + 1) // 2))
+
     def dp_at(k):
-        return lax.rem(me + k, n_dp)
+        x, z = me // RING_Z, lax.rem(me, RING_Z)
+        x = lax.rem(x + outward(k // RING_Z, n_dp // RING_Z), n_dp // RING_Z)
+        z = lax.rem(z + outward(lax.rem(k, RING_Z), RING_Z), RING_Z)
+        return x * RING_Z + z
 
     def ex_at(k):
         return lax.rem(ex + k, n_ex)
+
+    barrier = pltpu.get_barrier_semaphore()
+
+    @pl.loop(0, n_dp - 1)
+    def _(k):
+        pl.semaphore_signal(barrier, inc=1, device_id=(ex, dp_at(k)), device_id_type=MESH)
+
+    @pl.loop(1, n_ex)
+    def _(k):
+        pl.semaphore_signal(barrier, inc=1, device_id=(ex_at(k), me), device_id_type=MESH)
 
     loads = [
         pltpu.make_async_copy(src, dst, in_sem.at[n])
@@ -61,16 +78,6 @@
             pltpu.make_async_copy(grad_hbm.at[rows], grad.at[rows], pair_sem.at[0, c]),
             pltpu.make_async_copy(pout_hbm.at[cols], pout.at[cols], pair_sem.at[1, c]),
         )
-
-    barrier = pltpu.get_barrier_semaphore()
-
-    @pl.loop(1, n_dp)
-    def _(k):
-        pl.semaphore_signal(barrier, inc=1, device_id=(ex, dp_at(k)), device_id_type=MESH)
-
-    @pl.loop(1, n_ex)
-    def _(k):
-        pl.semaphore_signal(barrier, inc=1, device_id=(ex_at(k), me), device_id_type=MESH)
 
     @pl.loop(0, 8)
     def _(c):
@@ -141,7 +148,7 @@
     def val_dst():
         return raw.at[pl.ds(me * 4, 4)]
 
-    @pl.loop(1, n_dp)
+    @pl.loop(0, n_dp - 1)
     def _(k):
         to = dp_at(k)
         pltpu.make_async_remote_copy(
@@ -184,7 +191,7 @@
     def pair(ref, at):
         return ref.at[:, pl.ds(at * 2, 2), :]
 
-    @pl.loop(1, n_dp)
+    @pl.loop(0, n_dp - 1)
     def _(k):
         to = dp_at(k)
         pltpu.make_async_remote_copy(
@@ -213,7 +220,7 @@
     def two(ref, at):
         return ref.at[pl.ds(at * 2, 2), :]
 
-    @pl.loop(1, n_dp)
+    @pl.loop(0, n_dp - 1)
     def _(k):
         to = dp_at(k)
         pltpu.make_async_remote_copy(
@@ -284,7 +291,7 @@
         ]
         + [dma] * 10,
         compiler_params=pltpu.CompilerParams(
-            collective_id=0, has_side_effects=True, vmem_limit_bytes=48 << 20
+            collective_id=0, has_side_effects=True, vmem_limit_bytes=60 << 20
         ),
     )(
         tokens,

time: 50.7 us -> 44.1 us (0.87)
  local copies, waits for them, and re-layouts: 7.22 us -> 0 us
  other arithmetic: 0.56 us -> 1.24 us
    unnamed x14 -> x0, local copies, waits for them, and re-layouts: 7.22 us -> none
    mul x1, other arithmetic: 0.56 us -> 1.24 us  [body(): return summed * (1.0 / jnp.sqrt(F32(entries)))]
where the time goes in v2:
time: 44.1 us; the launch traced here: 44 us
  Pallas kernels  42.7 us (97%)
  other arithmetic  1.24 us (3%)
    pallas_call x1, Pallas kernels, body(): pl.pallas_call(functools.partial(kernel, n_dp, n_ex), out_shape=jax.Shape...  42.7 us
    mul x1, other arithmetic, body(): return summed * (1.0 / jnp.sqrt(F32(entries)))  1.24 us

profile of v2, /device:TPU:1, one launch (start us, length us, event | category | flops | bytes accessed | tf_op | source)
XLA Modules:
  0.0 44.0 jit_solution(13915925729814254632)
XLA Ops:
  0.0 42.7 %shard_map.82 = f32[2,128]{1,0:T(2,128)} custom-call(bf16[128,4096]{1,0:T(8,128)(2,1)} %tok_hbm.1, f32[8,128]{1,0:T(8,128)} %bitcast.11, s32[8,128]{1,0:T(8,128)} %bitcast.12, s32[1,128]{1,0:T(1,128)} %bitcast.13, bf16[2048,1536]{1,0:T(8,128)(2,1)} %bitcast.8, bf16[64,4096]{1,0:T(8,128)(2,1)} %bitcast.10, bf16[1024,1536]{1,0:T(8,128)(2,1)} %bitcast.9, ...), custom_call_target="tpu_custom_call" | custom-call | tf_op jit(solution)/shard_map/pallas_call | solution.py:263
  42.7 1.2 %broadcast_multiply_fusion = f32[2,128]{1,0:T(2,128)} fusion(f32[2,128]{1,0:T(2,128)} %shard_map.82), kind=kLoop, calls=%fused_computation | loop fusion | flops 256 | bytes 2048 | tf_op jit(solution)/shard_map/mul | solution.py:306

commit v3 on v2

--- a/solution.py
+++ b/solution.py
@@ -209,25 +209,31 @@
         at = pl.ds(pl.multiple_of(b * 16, 16), 16)
         turned = dot(swap, raw[at].reshape(256, 128)).astype(BF)
         for e in range(16):
-            vals[e, at, :] = turned[e * 16 : e * 16 + 16, :]
+            vals[e // 2, at, e % 2 * 128 : e % 2 * 128 + 128] = turned[e * 16 : e * 16 + 16, :]
 
     whole(train, train_r)
     score = jnp.zeros((64, 128), F32)
-    for e in range(16):
-        score += dot_nt(train[e], vals[e])
+    for c in range(8):
+        score += dot_nt(jnp.concatenate([train[2 * c], train[2 * c + 1]], axis=1), vals[c])
     part[...] = score
 
     def two(ref, at):
         return ref.at[pl.ds(at * 2, 2), :]
 
-    @pl.loop(0, n_dp - 1)
-    def _(k):
-        to = dp_at(k)
-        pltpu.make_async_remote_copy(
-            two(part, to), two(owned, me), part_s, part_r, device_id=(ex, to), device_id_type=MESH
-        ).start()
-
-    pltpu.make_async_copy(two(part, me), two(owned, me), part_r).start()
+    @pl.loop(0, n_dp)
+    def _(k):
+        to = lax.rem(k, n_dp // RING_Z) * RING_Z + k // (n_dp // RING_Z)
+
+        @pl.when(to != me)
+        def _():
+            pltpu.make_async_remote_copy(
+                two(part, to), two(owned, me), part_s, part_r, device_id=(ex, to), device_id_type=MESH
+            ).start()
+
+        @pl.when(to == me)
+        def _():
+            pltpu.make_async_copy(two(part, me), two(owned, me), part_r).start()
+
     whole(owned, part_r)
 
     def folded(value):
@@ -239,11 +245,15 @@
         rows += owned[8 * n : 8 * n + 8, :]
     mine[...] = folded(rows)
 
-    @pl.loop(1, n_ex)
-    def _(k):
-        pltpu.make_async_remote_copy(
-            mine.at[0:2, :], two(total, ex), own_s, own_r, device_id=(ex_at(k), me), device_id_type=MESH
-        ).start()
+    @pl.loop(0, n_ex)
+    def _(k):
+        to = jnp.where(k < 2, 1 - k, k)
+
+        @pl.when(to != ex)
+        def _():
+            pltpu.make_async_remote_copy(
+                mine.at[0:2, :], two(total, ex), own_s, own_r, device_id=(to, me), device_id_type=MESH
+            ).start()
 
     pltpu.make_async_copy(mine.at[0:2, :], two(total, ex), own_r).start()
     whole(total, own_r)
@@ -280,7 +290,7 @@
             pltpu.VMEM((2, 1024, 512), BF),
             pltpu.VMEM((16, 64, 128), BF),
             pltpu.VMEM((128, 16, 128), BF),
-            pltpu.VMEM((16, 128, 128), BF),
+            pltpu.VMEM((8, 128, 256), BF),
             pltpu.VMEM((16, 64, 128), BF),
             pltpu.VMEM((64, 128), F32),
             pltpu.VMEM((64, 128), F32),

time: 44.1 us -> 43.7 us (level)
  no operation moved by 1% of the time
where the time goes in v3:
time: 43.7 us; the launch traced here: 43.6 us
  Pallas kernels  42.4 us (97%)
  other arithmetic  1.24 us (3%)
    pallas_call x1, Pallas kernels, body(): pl.pallas_call(functools.partial(kernel, n_dp, n_ex), out_shape=jax.Shape...  42.4 us
    mul x1, other arithmetic, body(): return summed * (1.0 / jnp.sqrt(F32(entries)))  1.24 us

profile of v3, /device:TPU:1, one launch (start us, length us, event | category | flops | bytes accessed | tf_op | source)
XLA Modules:
  0.0 43.6 jit_solution(18034493581975695012)
XLA Ops:
  0.0 42.4 %shard_map.82 = f32[2,128]{1,0:T(2,128)} custom-call(bf16[128,4096]{1,0:T(8,128)(2,1)} %tok_hbm.1, f32[8,128]{1,0:T(8,128)} %bitcast.11, s32[8,128]{1,0:T(8,128)} %bitcast.12, s32[1,128]{1,0:T(1,128)} %bitcast.13, bf16[2048,1536]{1,0:T(8,128)(2,1)} %bitcast.8, bf16[64,4096]{1,0:T(8,128)(2,1)} %bitcast.10, bf16[1024,1536]{1,0:T(8,128)(2,1)} %bitcast.9, ...), custom_call_target="tpu_custom_call" | custom-call | tf_op jit(solution)/shard_map/pallas_call | solution.py:273
  42.4 1.2 %broadcast_multiply_fusion = f32[2,128]{1,0:T(2,128)} fusion(f32[2,128]{1,0:T(2,128)} %shard_map.82), kind=kLoop, calls=%fused_computation | loop fusion | flops 256 | bytes 2048 | tf_op jit(solution)/shard_map/mul | solution.py:316

commit v4 on v3

--- a/solution.py
+++ b/solution.py
@@ -97,10 +97,6 @@
     slots[...] = jnp.where(named > 0.0, dot(named.astype(BF), earlier), -1.0)
     gated[...] = weight
 
-    @pl.loop(0, 16)
-    def _(r):
-        diag[:, pl.ds(pl.multiple_of(r * 64, 64), 64), :] = jnp.zeros((2, 64, 512), BF)
-
     for load in loads[3:]:
         load.wait()
     act = dot_nt(pin[...], tok[...])
@@ -112,6 +108,23 @@
     x_hi = jnp.where(member, dot(spread, act_hi), 0.0).astype(BF)
     x_lo = jnp.where(member, dot(spread, act_lo), 0.0).astype(BF)
 
+    x_both = jnp.concatenate([x_hi, x_lo], axis=1)
+
+    pl.semaphore_wait(barrier, n_dp - 1 + n_ex - 1)
+
+    def val_src(to):
+        return val_hbm.at[:, :, pl.ds(pl.multiple_of(to * 128, 128), 128)]
+
+    def val_dst():
+        return raw.at[pl.ds(me * 4, 4)]
+
+    @pl.loop(0, 20)
+    def _(k):
+        to = dp_at(k)
+        pltpu.make_async_remote_copy(
+            val_src(to), val_dst(), val_s, val_r, device_id=(ex, to), device_id_type=MESH
+        ).start()
+
     place = iota((16, 128), 0).astype(F32)
 
     @pl.loop(0, n_ex)
@@ -123,12 +136,10 @@
         pick = jnp.concatenate(blocks, axis=0)
         pick_hi = pick.astype(BF)
         pick_lo = (pick - pick_hi.astype(F32)).astype(BF)
-        y = dot_nt(x_hi, pick_hi) + dot_nt(x_lo, pick_hi) + dot_nt(x_hi, pick_lo)
+        y = dot_nt(x_both, jnp.concatenate([pick_hi, pick_hi], axis=1)) + dot_nt(x_hi, pick_lo)
         y = y.astype(BF)
         ysend[g, 0] = y[:, :128]
         ysend[g, 1] = y[:, 128:]
-
-    pl.semaphore_wait(barrier, n_dp - 1 + n_ex - 1)
 
     def act_dst():
         return yrecv.at[:, :, pl.ds(pl.multiple_of(ex * 128, 128), 128)]
@@ -142,13 +153,7 @@
 
     pltpu.make_async_copy(ysend.at[ex], act_dst(), act_r).start()
 
-    def val_src(to):
-        return val_hbm.at[:, :, pl.ds(pl.multiple_of(to * 128, 128), 128)]
-
-    def val_dst():
-        return raw.at[pl.ds(me * 4, 4)]
-
-    @pl.loop(0, n_dp - 1)
+    @pl.loop(20, n_dp - 1)
     def _(k):
         to = dp_at(k)
         pltpu.make_async_remote_copy(
@@ -156,6 +161,10 @@
         ).start()
 
     pltpu.make_async_copy(val_src(me), val_dst(), val_r).start()
+
+    @pl.loop(0, 16)
+    def _(r):
+        diag[:, pl.ds(pl.multiple_of(r * 64, 64), 64), :] = jnp.zeros((2, 64, 512), BF)
 
     own_half = (iota((256, 128), 0) // 128) == (iota((256, 128), 1) // 64)
 

time: 43.7 us -> 43.2 us (0.989)
  Pallas kernels: 42.4 us -> 41.8 us
    pallas_call x1, Pallas kernels: 42.4 us -> 41.8 us  [body(): pl.pallas_call(functools.partial(kernel, n_dp, n_ex), out_shape=jax.Shape...]
where the time goes in v4:
time: 43.2 us; the launch traced here: 43 us
  Pallas kernels  41.8 us (97%)
  other arithmetic  1.24 us (3%)
    pallas_call x1, Pallas kernels, body(): pl.pallas_call(functools.partial(kernel, n_dp, n_ex), out_shape=jax.Shape...  41.8 us
    mul x1, other arithmetic, body(): return summed * (1.0 / jnp.sqrt(F32(entries)))  1.24 us

profile of v4, /device:TPU:1, one launch (start us, length us, event | category | flops | bytes accessed | tf_op | source)
XLA Modules:
  0.0 43.0 jit_solution(11209044717540889503)
XLA Ops:
  0.0 41.8 %shard_map.82 = f32[2,128]{1,0:T(2,128)} custom-call(bf16[128,4096]{1,0:T(8,128)(2,1)} %tok_hbm.1, f32[8,128]{1,0:T(8,128)} %bitcast.11, s32[8,128]{1,0:T(8,128)} %bitcast.12, s32[1,128]{1,0:T(1,128)} %bitcast.13, bf16[2048,1536]{1,0:T(8,128)(2,1)} %bitcast.8, bf16[64,4096]{1,0:T(8,128)(2,1)} %bitcast.10, bf16[1024,1536]{1,0:T(8,128)(2,1)} %bitcast.9, ...), custom_call_target="tpu_custom_call" | custom-call | tf_op jit(solution)/shard_map/pallas_call | solution.py:282
  41.8 1.2 %broadcast_multiply_fusion = f32[2,128]{1,0:T(2,128)} fusion(f32[2,128]{1,0:T(2,128)} %shard_map.82), kind=kLoop, calls=%fused_computation | loop fusion | flops 256 | bytes 2048 | tf_op jit(solution)/shard_map/mul | solution.py:325

commit v5 on v4

--- a/solution.py
+++ b/solution.py
@@ -83,6 +83,21 @@
     def _(c):
         for load in pair_loads(c):
             load.start()
+
+    pl.semaphore_wait(barrier, n_dp - 1 + n_ex - 1)
+
+    def val_src(to):
+        return val_hbm.at[:, :, pl.ds(pl.multiple_of(to * 128, 128), 128)]
+
+    def val_dst():
+        return raw.at[pl.ds(me * 4, 4)]
+
+    @pl.loop(0, 20)
+    def _(k):
+        to = dp_at(k)
+        pltpu.make_async_remote_copy(
+            val_src(to), val_dst(), val_s, val_r, device_id=(ex, to), device_id_type=MESH
+        ).start()
 
     for load in loads[:3]:
         load.wait()
@@ -109,21 +124,6 @@
     x_lo = jnp.where(member, dot(spread, act_lo), 0.0).astype(BF)
 
     x_both = jnp.concatenate([x_hi, x_lo], axis=1)
-
-    pl.semaphore_wait(barrier, n_dp - 1 + n_ex - 1)
-
-    def val_src(to):
-        return val_hbm.at[:, :, pl.ds(pl.multiple_of(to * 128, 128), 128)]
-
-    def val_dst():
-        return raw.at[pl.ds(me * 4, 4)]
-
-    @pl.loop(0, 20)
-    def _(k):
-        to = dp_at(k)
-        pltpu.make_async_remote_copy(
-            val_src(to), val_dst(), val_s, val_r, device_id=(ex, to), device_id_type=MESH
-        ).start()
 
     place = iota((16, 128), 0).astype(F32)
 
@@ -229,20 +229,16 @@
     def two(ref, at):
         return ref.at[pl.ds(at * 2, 2), :]
 
-    @pl.loop(0, n_dp)
-    def _(k):
+    @pl.loop(0, n_dp - 1)
+    def _(k):
+        turn = me % RING_Z * (n_dp // RING_Z) + me // RING_Z
+        k = jnp.where(k >= turn, k + 1, k)
         to = lax.rem(k, n_dp // RING_Z) * RING_Z + k // (n_dp // RING_Z)
-
-        @pl.when(to != me)
-        def _():
-            pltpu.make_async_remote_copy(
-                two(part, to), two(owned, me), part_s, part_r, device_id=(ex, to), device_id_type=MESH
-            ).start()
-
-        @pl.when(to == me)
-        def _():
-            pltpu.make_async_copy(two(part, me), two(owned, me), part_r).start()
-
+        pltpu.make_async_remote_copy(
+            two(part, to), two(owned, me), part_s, part_r, device_id=(ex, to), device_id_type=MESH
+        ).start()
+
+    pltpu.make_async_copy(two(part, me), two(owned, me), part_r).start()
     whole(owned, part_r)
 
     def folded(value):

time: 43.2 us -> 43.1 us (level)
  no operation moved by 1% of the time
where the time goes in v5:
time: 43.1 us; the launch traced here: 43 us
  Pallas kernels  41.7 us (97%)
  other arithmetic  1.24 us (3%)
    pallas_call x1, Pallas kernels, body(): pl.pallas_call(functools.partial(kernel, n_dp, n_ex), out_shape=jax.Shape...  41.7 us
    mul x1, other arithmetic, body(): return summed * (1.0 / jnp.sqrt(F32(entries)))  1.24 us

profile of v5, /device:TPU:1, one launch (start us, length us, event | category | flops | bytes accessed | tf_op | source)
XLA Modules:
  0.0 43.0 jit_solution(15625002263791325733)
XLA Ops:
  0.0 41.7 %shard_map.82 = f32[2,128]{1,0:T(2,128)} custom-call(bf16[128,4096]{1,0:T(8,128)(2,1)} %tok_hbm.1, f32[8,128]{1,0:T(8,128)} %bitcast.11, s32[8,128]{1,0:T(8,128)} %bitcast.12, s32[1,128]{1,0:T(1,128)} %bitcast.13, bf16[2048,1536]{1,0:T(8,128)(2,1)} %bitcast.8, bf16[64,4096]{1,0:T(8,128)(2,1)} %bitcast.10, bf16[1024,1536]{1,0:T(8,128)(2,1)} %bitcast.9, ...), custom_call_target="tpu_custom_call" | custom-call | tf_op jit(solution)/shard_map/pallas_call | solution.py:278
  41.7 1.2 %broadcast_multiply_fusion = f32[2,128]{1,0:T(2,128)} fusion(f32[2,128]{1,0:T(2,128)} %shard_map.82), kind=kLoop, calls=%fused_computation | loop fusion | flops 256 | bytes 2048 | tf_op jit(solution)/shard_map/mul | solution.py:321

commit v6 on v5

--- a/solution.py
+++ b/solution.py
@@ -92,7 +92,7 @@
     def val_dst():
         return raw.at[pl.ds(me * 4, 4)]
 
-    @pl.loop(0, 20)
+    @pl.loop(0, 12)
     def _(k):
         to = dp_at(k)
         pltpu.make_async_remote_copy(
@@ -153,7 +153,7 @@
 
     pltpu.make_async_copy(ysend.at[ex], act_dst(), act_r).start()
 
-    @pl.loop(20, n_dp - 1)
+    @pl.loop(12, n_dp - 1)
     def _(k):
         to = dp_at(k)
         pltpu.make_async_remote_copy(

time: 43.1 us -> 43 us (level)
  no operation moved by 1% of the time
where the time goes in v6:
time: 43 us; the launch traced here: 42.9 us
  Pallas kernels  41.7 us (97%)
  other arithmetic  1.24 us (3%)
    pallas_call x1, Pallas kernels, body(): pl.pallas_call(functools.partial(kernel, n_dp, n_ex), out_shape=jax.Shape...  41.7 us
    mul x1, other arithmetic, body(): return summed * (1.0 / jnp.sqrt(F32(entries)))  1.24 us

profile of v6, /device:TPU:1, one launch (start us, length us, event | category | flops | bytes accessed | tf_op | source)
XLA Modules:
  0.0 42.9 jit_solution(14989830296433584586)
XLA Ops:
  0.0 41.7 %shard_map.82 = f32[2,128]{1,0:T(2,128)} custom-call(bf16[128,4096]{1,0:T(8,128)(2,1)} %tok_hbm.1, f32[8,128]{1,0:T(8,128)} %bitcast.11, s32[8,128]{1,0:T(8,128)} %bitcast.12, s32[1,128]{1,0:T(1,128)} %bitcast.13, bf16[2048,1536]{1,0:T(8,128)(2,1)} %bitcast.8, bf16[64,4096]{1,0:T(8,128)(2,1)} %bitcast.10, bf16[1024,1536]{1,0:T(8,128)(2,1)} %bitcast.9, ...), custom_call_target="tpu_custom_call" | custom-call | tf_op jit(solution)/shard_map/pallas_call | solution.py:278
  41.7 1.2 %broadcast_multiply_fusion = f32[2,128]{1,0:T(2,128)} fusion(f32[2,128]{1,0:T(2,128)} %shard_map.82), kind=kLoop, calls=%fused_computation | loop fusion | flops 256 | bytes 2048 | tf_op jit(solution)/shard_map/mul | solution.py:321
